TPU v7x, 128 devices: a whole 4x4x4 slice. The times are simulated.
128 devices in a mesh: row: 16 (over y, z), col: 8 (over x, core).
Axes of the slice: x: 4, y: 4, z: 4, core: 2. Of those that a mesh axis runs over, the one named last changes fastest.
Arguments:
- matrix: float32 [18432, 18432], P('row', 'col'), as said below
Outputs:
- updated: float32 [18432, 18432], P('row', 'col')
- reflectors: float32 [18432, 512], P('row')
Inputs may be any that keep to these rules, and one draw needn't show every extreme that they name: matrix is symmetric.
All inputs are finite; a program needn't handle non-finite values.
Results may differ from a plain program's by a relative error of at most 0.00016.
Values sent between devices are 32-bit elements; how exact they have to be, the bound alone decides.
A program may use at most 128 MiB of HBM per device.

v0:
```python
import jax
import jax.numpy as jnp
from jax import lax
from jax.sharding import PartitionSpec as P

BAND = 256
PANELS = 2
HIGH = lax.Precision.HIGHEST


def mm(a, b):
    return jnp.dot(a, b, precision=HIGH)


def mm_tn(a, b):
    return lax.dot_general(a, b, (((0,), (0,)), ((), ())), precision=HIGH)


def mm_nt(a, b):
    return lax.dot_general(a, b, (((1,), (1,)), ((), ())), precision=HIGH)


def transpose_exchange(x, rows, cols):
    both = ("row", "col")
    first = []
    second = []
    for s in range(rows):
        for j in range(cols):
            src = s * cols + j
            first.append((src, (2 * j + s % 2) * cols + s // 2))
            second.append((src, (2 * j + 1 - s % 2) * cols + s // 2))
    got1 = lax.ppermute(x, both, first)
    got2 = lax.ppermute(x, both, second)
    odd_row = lax.axis_index("row") % 2 == 1
    even = jnp.where(odd_row, got2, got1)
    odd = jnp.where(odd_row, got1, got2)
    return jnp.concatenate([even, odd], axis=0)


def small_factors(gram, top):
    identity = jnp.eye(BAND, dtype=jnp.float32)
    low = jnp.linalg.cholesky(gram)
    low_inv = jax.scipy.linalg.solve_triangular(low, identity, lower=True)
    shifted = identity + mm_nt(top, low_inv)
    second = jnp.linalg.cholesky(mm_nt(shifted, shifted))
    second_inv = jax.scipy.linalg.solve_triangular(second, identity, lower=True)
    transform = mm_tn(shifted, mm_tn(second_inv, second_inv))
    return (low_inv, transform)


def body(a):
    rows = lax.psum(1, "row")
    cols = lax.psum(1, "col")
    row_count, col_count = a.shape
    r = lax.axis_index("row")
    c = lax.axis_index("col")
    row_pos = r * row_count + jnp.arange(row_count, dtype=jnp.int32)
    col_pos = c * col_count + jnp.arange(col_count, dtype=jnp.int32)
    band_idx = jnp.arange(BAND, dtype=jnp.int32)
    width = PANELS * BAND
    col_zero = c == 0
    colb = lax.psum(jnp.where(col_zero, a[:, :width], 0.0), "col")
    strip_t = transpose_exchange(colb, rows, cols)
    lo = BAND
    p0_loc = jnp.where(row_pos[:, None] >= lo, a[:, :BAND], 0.0)
    g_loc = jnp.where(col_zero, mm_tn(p0_loc, p0_loc), 0.0)
    top_loc = jnp.where(col_zero & (r == 0), a[lo : lo + BAND, :BAND], 0.0)
    gram0, top0 = lax.psum((g_loc, top_loc), ("row", "col"))
    stored = []
    current = a
    prev = None
    for k in range(PANELS):
        lo = (k + 1) * BAND
        if k == 0:
            gram, top = (gram0, top0)
            pr = jnp.where(row_pos[:, None] >= lo, colb[:, :BAND], 0.0)
            pc = jnp.where(col_pos[:, None] >= lo, strip_t[:, :BAND], 0.0)
        else:
            y_r0, w_r0, y_c0, w_c0, y_e0, w_e0 = prev
            pr = colb[:, k * BAND : (k + 1) * BAND] - mm_nt(y_r0, w_e0) - mm_nt(w_r0, y_e0)
            pc = strip_t[:, k * BAND : (k + 1) * BAND] - mm_nt(y_c0, w_e0) - mm_nt(w_c0, y_e0)
            pr = jnp.where(row_pos[:, None] >= lo, pr, 0.0)
            pc = jnp.where(col_pos[:, None] >= lo, pc, 0.0)
            g_part = mm_tn(pc, pc)
            top_part = jnp.where(col_zero, pc[lo : lo + BAND], 0.0)
            gram, top = lax.psum((g_part, top_part), "col")
        low_inv, transform = small_factors(gram, top)
        unit_r = (row_pos[:, None] - lo == band_idx[None, :]).astype(jnp.float32)
        unit_c = (col_pos[:, None] - lo == band_idx[None, :]).astype(jnp.float32)
        y_r = mm_nt(pr, low_inv) + unit_r
        y_c = mm_nt(pc, low_inv) + unit_c
        stored.append(y_r)
        xp = mm(current, y_c)
        if k + 1 < PANELS:
            nlo = (k + 1) * BAND
            ext = mm_tn(strip_t[:, nlo : nlo + BAND], y_c)
            x_r, x_e = lax.psum((xp, ext), "col")
        else:
            x_r = lax.psum(xp, "col")
        curv = lax.psum(mm_tn(y_r, xp), ("row", "col"))
        x_c = transpose_exchange(x_r, rows, cols)
        middle = mm_nt(mm(transform, curv), transform)
        w_r = mm_nt(x_r, transform) - 0.5 * mm(y_r, middle)
        w_c = mm_nt(x_c, transform) - 0.5 * mm(y_c, middle)
        current = current - mm_nt(y_r, w_c) - mm_nt(w_r, y_c)
        if k + 1 < PANELS:
            y_e = mm_nt(top, low_inv) + jnp.eye(BAND, dtype=jnp.float32)
            w_e = mm_nt(x_e, transform) - 0.5 * mm(y_e, middle)
            prev = (y_r, w_r, y_c, w_c, y_e, w_e)
    return (current, jnp.concatenate(stored, axis=1))


def solution(mesh):
    return jax.shard_map(
        body,
        mesh=mesh,
        in_specs=(P("row", "col"),),
        out_specs=(P("row", "col"), P("row", None)),
        check_vma=False,
    )
```

profile of v0, /device:TPU:1, one launch (start us, length us, event | category | flops | bytes accessed | tf_op | source)
XLA Modules:
  0.0 1369.1 jit_solution(15635334820634010336)
XLA Ops:
  8.8 2.0 fusion.18
  12.5 1.9 copy.20
  21.0 137.2 %all-reduce.14.cloned.1.call-done = f32[256,256]{0,1:T(8,128)} async-done(((f32[256,256]{0,1:T(8,128)}), f32[256,256]{0,1:T(8,128)}) %all-reduce.14.cloned.1.call-update) | async-done | bytes 262160 | tf_op jit(solution)/shard_map/psum | solution.py:68
  160.3 11.7 cholesky.214
  172.0 9.8 custom-call.17
  182.1 41.3 %all-reduce.12.cloned.1.call-done = f32[1152,512]{0,1:T(8,128)} async-done(((f32[1152,512]{0,1:T(8,128)}), f32[1152,512]{0,1:T(8,128)}) %all-reduce.12.cloned.1.call-update) | async-done | bytes 2359312 | tf_op jit(solution)/shard_map/psum | solution.py:62
  223.4 7.2 collective-permute-start.1
  231.2 11.7 cholesky.231
  245.0 4.0 while.8
  249.6 19.7 %custom-call.18 = f32[2,128,128]{1,2,0:T(8,128)S(1)} custom-call(f32[2,128,128]{2,1,0:T(8,128)S(1)} %get-tuple-element.30), custom_call_target="InvertDiagBlocksLowerTriangular" | custom-call | tf_op jit(solution)/shard_map/jit(_solve_triangular)/triangular_solve | solution.py:43
  270.2 2.7 convolution_add_fusion.3
  272.9 9.8 collective-permute-done
  282.7 2.7 broadcast_select_fusion.1
  285.4 4.2 convolution_add_fusion.1
  289.7 21.5 %fusion.94 = f32[256,1152]{1,0:T(8,128)S(1)} fusion(f32[2304,256]{1,0:T(8,128)S(1)} %convolution_add_fusion.1, f32[1152,2304]{1,0:T(8,128)} %param.4), kind=kOutput, calls=%fused_computation.198 | convolution fusion | flops 8153726976 | bytes 14155776 | tf_op jit(solution)/shard_map/dot_general | solution.py:12
  312.2 1.9 fusion.97
  314.2 4.5 fusion.22
  318.9 293.3 %all-reduce.20.cloned.1.call-done = (f32[256,256]{0,1:T(8,128)}, f32[256,256]{1,0:T(8,128)}) async-done(((f32[256,256]{0,1:T(8,128)}, f32[256,256]{1,0:T(8,128)}), (f32[256,256]{0,1:T(8,128)}, f32[256,256]{1,0:T(8,128)})) %all-reduce.20.cloned.1.call-update) | async-done | bytes 524304 | tf_op jit(solution)/shard_map/psum | solution.py:68
  619.9 13.2 cholesky.248
  635.2 11.3 custom-call.19
  651.5 13.2 cholesky.265
  670.4 7.2 while.9
  671.3 2.9 bitcast_dynamic-update-slice_fusion.9
  674.8 2.8 bitcast_dynamic-update-slice_fusion.9
  677.6 21.1 %custom-call.20 = f32[2,128,128]{1,2,0:T(8,128)} custom-call(f32[2,128,128]{2,1,0:T(8,128)} %get-tuple-element.31), custom_call_target="InvertDiagBlocksLowerTriangular" | custom-call | tf_op jit(solution)/shard_map/jit(_solve_triangular)/triangular_solve | solution.py:46
  706.4 3.4 convolution_multiply_fusion.1
  709.8 3.5 fusion.100
  713.3 4.2 collective-permute-start.3
  719.8 2.0 fusion.4
  723.3 2.5 fusion.3
  725.7 18.9 %collective-permute-done.3 = f32[1152,256]{0,1:T(8,128)S(1)} collective-permute-done((f32[1152,256]{0,1:T(8,128)S(1)}, f32[1152,256]{0,1:T(8,128)S(1)}, u32[]{:S(2)}, u32[]{:S(2)}) %collective-permute-start.3) | collective-permute-done | bytes 1179680 | tf_op jit(solution)/shard_map/ppermute | solution.py:32
  746.4 4.1 convolution_subtract_fusion.6
  750.4 2.3 fusion.102
  752.8 19.4 %convolution_subtract_fusion.3 = f32[1152,2304]{1,0:T(8,128)} fusion(f32[1152,2304]{1,0:T(8,128)S(1)} %bitcast.193, f32[1152,256]{0,1:T(8,128)S(1)} %convolution_add_fusion.3, f32[2304,256]{1,0:T(8,128)S(1)} %convolution_subtract_fusion.6), kind=kOutput, calls=%fused_computation.11 | convolution fusion | flops 8156381184 | bytes 24772608 | tf_op jit(solution)/shard_map/dot_general | solution.py:20
  772.2 2.6 fusion.1
  776.2 2.8 fusion.103
  779.0 13.9 %convolution_subtract_fusion.2 = f32[1152,2304]{1,0:T(8,128)} fusion(f32[1152,2304]{1,0:T(8,128)} %convolution_subtract_fusion.3, f32[1152,256]{1,0:T(8,128)} %copy-done.13, f32[2304,256]{1,0:T(8,128)S(1)} %convolution_add_fusion.1), kind=kOutput, calls=%fused_computation.10 | convolution fusion | flops 8156381184 | bytes 24772608 | tf_op jit(solution)/shard_map/dot_general | solution.py:20
  794.7 116.0 %all-reduce.16.cloned.1.call-done = f32[256,256]{0,1:T(8,128)} async-done(((f32[256,256]{0,1:T(8,128)}), f32[256,256]{0,1:T(8,128)}) %all-reduce.16.cloned.1.call-update) | async-done | bytes 262160 | tf_op jit(solution)/shard_map/psum | solution.py:86
  915.0 13.2 cholesky.282
  930.3 11.3 custom-call.21
  946.6 13.2 cholesky.299
  965.5 6.8 while.10
  966.1 2.8 bitcast_dynamic-update-slice_fusion.10
  969.5 2.8 bitcast_dynamic-update-slice_fusion.10
  972.3 21.3 %custom-call.22 = f32[2,128,128]{1,2,0:T(8,128)} custom-call(f32[2,128,128]{2,1,0:T(8,128)} %get-tuple-element.32), custom_call_target="InvertDiagBlocksLowerTriangular" | custom-call | tf_op jit(solution)/shard_map/jit(_solve_triangular)/triangular_solve | solution.py:43
  997.9 4.4 convolution_add_fusion
  1003.7 11.2 fusion.104
  1016.4 2.6 convolution_add_fusion.2
  1020.8 3.0 copy.15
  1023.8 1.9 fusion.107
  1025.8 53.7 %all-reduce.22.cloned.1.call-done = (f32[256,256]{0,1:T(8,128)}, f32[1152,256]{0,1:T(8,128)}) async-done(((f32[256,256]{0,1:T(8,128)}, f32[1152,256]{0,1:T(8,128)}), (f32[256,256]{0,1:T(8,128)}, f32[1152,256]{0,1:T(8,128)})) %all-reduce.22.cloned.1.call-update) | async-done | bytes 1441808 | tf_op jit(solution)/shard_map/psum | solution.py:86
  1079.4 7.2 collective-permute-start.5
  1089.4 11.7 cholesky.316
  1101.8 9.8 custom-call.23
  1112.1 11.7 cholesky.333
  1126.0 4.2 while.11
  1130.3 19.8 %custom-call.24 = f32[2,128,128]{1,2,0:T(8,128)S(1)} custom-call(f32[2,128,128]{2,1,0:T(8,128)S(1)} %get-tuple-element.33), custom_call_target="InvertDiagBlocksLowerTriangular" | custom-call | tf_op jit(solution)/shard_map/jit(_solve_triangular)/triangular_solve | solution.py:46
  1152.3 163.1 %all-reduce.18.cloned.1.call-done = f32[256,256]{1,0:T(8,128)} async-done(((f32[256,256]{1,0:T(8,128)}), f32[256,256]{1,0:T(8,128)}) %all-reduce.18.cloned.1.call-update) | async-done | bytes 262160 | tf_op jit(solution)/shard_map/psum | solution.py:100
  1318.3 3.5 fusion.110
  1321.8 2.0 fusion.2
  1323.8 2.1 convolution_multiply_fusion
  1327.9 4.3 convolution_subtract_fusion.4
  1332.3 18.1 %convolution_subtract_fusion.1 = f32[1152,2304]{1,0:T(8,128)S(1)} fusion(f32[1152,2304]{1,0:T(8,128)S(1)} %bitcast.191, f32[1152,256]{0,1:T(8,128)S(1)} %copy-done.9, f32[2304,256]{1,0:T(8,128)S(1)} %convolution_subtract_fusion.4), kind=kOutput, calls=%fused_computation.9 | convolution fusion | flops 8156381184 | bytes 24772608 | tf_op jit(solution)/shard_map/dot_general | solution.py:20
  1350.3 11.5 convolution_subtract_fusion
  (239 shorter events, 98.7 us)
Async XLA Ops:
  7.2 1.3 slice-start.6
  7.2 151.0 %all-reduce.14.cloned.1.call-start = ((), (), s32[]{:S(2)}) async-start(), calls=%async_computation.1 | async-start | bytes 524288 | tf_op jit(solution)/shard_map/psum | solution.py:68
  10.8 1.7 slice-start.7
  10.8 212.5 %all-reduce.12.cloned.1.call-start = ((), (), s32[]{:S(2)}) async-start(), calls=%async_computation | async-start | bytes 4718592 | tf_op jit(solution)/shard_map/psum | solution.py:62
  16.0 596.2 %all-reduce.20.cloned.1.call-start = ((), (), s32[]{:S(2)}) async-start(), calls=%async_computation.4 | async-start | bytes 1048576 | tf_op jit(solution)/shard_map/psum | solution.py:68
  20.2 249.3 %copy-start.19 = (f32[256,256]{1,0:T(8,128)}, f32[256,256]{1,0:T(8,128)S(1)}, u32[]{:S(2)}) copy-start(f32[256,256]{1,0:T(8,128)S(1)} %fusion.39) | copy-start | bytes 786436
  223.4 49.5 %collective-permute-start.1 = (f32[1152,512]{0,1:T(8,128)}, f32[1152,512]{0,1:T(8,128)}, u32[]{:S(2)}, u32[]{:S(2)}) collective-permute-start(f32[1152,512]{0,1:T(8,128)} %all-reduce.12.cloned.1.call-done), channel_id=1, source_target_pairs={{0,0},{1,16},{2,32},{3,48},{4,64},{5,80},{6,96},{7,112},{8,8},{9,2... | collective-permute-start | bytes 7077896 | tf_op jit(solution)/shard_map/ppermute | solution.py:32
  230.6 52.1 %collective-permute-start = (f32[1152,512]{0,1:T(8,128)}, f32[1152,512]{0,1:T(8,128)}, u32[]{:S(2)}, u32[]{:S(2)}) collective-permute-start(f32[1152,512]{0,1:T(8,128)} %all-reduce.12.cloned.1.call-done), channel_id=1, source_target_pairs={{0,8},{1,24},{2,40},{3,56},{4,72},{5,88},{6,104},{7,120},{8,0},{9,... | collective-permute-start | bytes 7077896 | tf_op jit(solution)/shard_map/ppermute | solution.py:33
  249.0 0.6 copy-start.40
  269.6 15.8 %copy-start.23 = (f32[128,256]{1,0:T(8,128)}, f32[128,256]{1,0:T(8,128)S(1)}, u32[]{:S(2)}) copy-start(f32[128,256]{1,0:T(8,128)S(1)} %fusion.46) | copy-start | bytes 393220
  270.2 15.2 %copy-start.27 = (f32[128,256]{1,0:T(8,128)}, f32[128,256]{1,0:T(8,128)S(1)}, u32[]{:S(2)}) copy-start(f32[128,256]{1,0:T(8,128)S(1)} %fusion.61) | copy-start | bytes 393220
  272.9 12.6 copy-start.37
  285.4 4.3 copy-start.4
  285.4 4.3 copy-start.6
  311.2 1.0 copy-start.12
  314.2 395.6 %all-reduce.24.cloned.1.call-start = ((), (), s32[]{:S(2)}) async-start(), calls=%async_computation.6 | async-start | bytes 2883584 | tf_op jit(solution)/shard_map/psum | solution.py:97
  318.7 591.9 %all-reduce.16.cloned.1.call-start = ((), (), s32[]{:S(2)}) async-start(), calls=%async_computation.2 | async-start | bytes 524288 | tf_op jit(solution)/shard_map/psum | solution.py:86
  612.2 58.2 %copy-start.41 = (s32[2,2]{1,0:T(2,128)S(1)}, s32[2,2]{1,0:T(2,128)}, u32[]{:S(2)}) copy-start(s32[2,2]{1,0:T(2,128)} %copy-done.40) | copy-start | bytes 52
  613.9 0.7 copy-start.10
  618.6 0.7 copy-start.31
  698.7 5.8 copy-start.34
  704.5 0.7 copy-start.14
  705.7 0.7 copy-start.21
  709.8 3.5 copy-start.30
  709.8 9.2 copy-start.15
  709.8 9.2 copy-start.33
  709.8 9.6 copy-start.11
  709.8 9.6 copy-start.22
  713.3 31.4 %collective-permute-start.3 = (f32[1152,256]{0,1:T(8,128)S(1)}, f32[1152,256]{0,1:T(8,128)S(1)}, u32[]{:S(2)}, u32[]{:S(2)}) collective-permute-start(f32[1152,256]{0,1:T(8,128)S(1)} %copy-done.30), channel_id=1, source_target_pairs={{0,0},{1,16},{2,32},{3,48},{4,64},{5,80},{6,96},{7,112},{8,8},{9,2... | collective-permute-start | bytes 3538952 | tf_op jit(solution)/shard_map/ppermute | solution.py:32
  717.5 28.7 %collective-permute-start.2 = (f32[1152,256]{0,1:T(8,128)S(1)}, f32[1152,256]{0,1:T(8,128)S(1)}, u32[]{:S(2)}, u32[]{:S(2)}) collective-permute-start(f32[1152,256]{0,1:T(8,128)S(1)} %copy-done.30), channel_id=1, source_target_pairs={{0,8},{1,24},{2,40},{3,56},{4,72},{5,88},{6,104},{7,120},{8,0},{9,... | collective-permute-start | bytes 3538952 | tf_op jit(solution)/shard_map/ppermute | solution.py:33
  719.4 2.5 copy-start.26
  721.9 1.4 copy-start.13
  721.9 1.4 copy-start.39
  723.3 23.1 %copy-start.16 = (f32[2304,256]{1,0:T(8,128)S(1)}, f32[2304,256]{1,0:T(8,128)}, u32[]{:S(2)}) copy-start(f32[2304,256]{1,0:T(8,128)} %convolution_multiply_fusion.1) | copy-start | bytes 7077892
  723.3 29.5 %slice-start.3 = ((s8[10616832]{0:T(1024)(128)(4,1)}), s8[4194304]{0:T(1024)(128)(4,1)S(1)}, s32[]{:S(2)}) async-start(s8[10616832]{0:T(1024)(128)(4,1)} %bitcast.192), calls=%async_computation.10 | async-start | bytes 8388608
  725.7 27.0 %slice-start.4 = ((s8[10616832]{0:T(1024)(128)(4,1)}), s8[4194304]{0:T(1024)(128)(4,1)S(1)}, s32[]{:S(2)}) async-start(s8[10616832]{0:T(1024)(128)(4,1)} %bitcast.192), calls=%async_computation.11 | async-start | bytes 8388608
  746.4 6.4 slice-start.5
  752.8 19.4 %copy-start.5 = (f32[1152,512]{0,1:T(8,128)S(1)}, f32[1152,512]{0,1:T(8,128)}, u32[]{:S(2)}) copy-start(f32[1152,512]{0,1:T(8,128)} %copy-done.4) | copy-start | bytes 7077892
  752.8 19.4 %copy-start.7 = (f32[1152,512]{0,1:T(8,128)S(1)}, f32[1152,512]{0,1:T(8,128)}, u32[]{:S(2)}) copy-start(f32[1152,512]{0,1:T(8,128)} %copy-done.6) | copy-start | bytes 7077892
  752.8 19.4 %copy-start.38 = (pred[2304]{0:T(1024)(128)(4,1)S(1)}, pred[2304]{0:T(1024)(128)(4,1)}, u32[]{:S(2)}) copy-start(pred[2304]{0:T(1024)(128)(4,1)} %fusion.69) | copy-start | bytes 6916
  774.7 1.4 copy-start
  779.0 300.5 %all-reduce.22.cloned.1.call-start = ((), (), s32[]{:S(2)}) async-start(), calls=%async_computation.5 | async-start | bytes 2883584 | tf_op jit(solution)/shard_map/psum | solution.py:86
  912.4 85.5 %copy-start.1 = (f32[2304,256]{0,1:T(8,128)S(1)}, f32[2304,256]{0,1:T(8,128)}, u32[]{:S(2)}) copy-start(f32[2304,256]{0,1:T(8,128)} %copy-done) | copy-start | bytes 7077892
  912.4 85.5 %copy-start.35 = (s32[2304]{0:T(1024)S(1)}, s32[2304]{0:T(1024)}, u32[]{:S(2)}) copy-start(s32[2304]{0:T(1024)} %fusion.68) | copy-start | bytes 27652
  913.6 0.7 copy-start.32
  994.8 2.4 copy-start.24
  997.2 0.7 copy-start.28
  1002.3 1.4 copy-start.2
  1014.9 1.5 copy-start.36
  1016.3 299.0 %all-reduce.18.cloned.1.call-start = ((), (), s32[]{:S(2)}) async-start(), calls=%async_computation.3 | async-start | bytes 524288 | tf_op jit(solution)/shard_map/psum | solution.py:100
  1019.0 4.8 copy-start.8
  1023.8 63.4 %copy-start.25 = (f32[128,256]{1,0:T(8,128)S(1)}, f32[128,256]{1,0:T(8,128)}, u32[]{:S(2)}) copy-start(f32[128,256]{1,0:T(8,128)} %copy-done.24) | copy-start | bytes 393220
  1023.8 63.4 %copy-start.29 = (f32[128,256]{1,0:T(8,128)S(1)}, f32[128,256]{1,0:T(8,128)}, u32[]{:S(2)}) copy-start(f32[128,256]{1,0:T(8,128)} %copy-done.28) | copy-start | bytes 393220
  1079.4 246.6 %collective-permute-start.5 = (f32[1152,256]{0,1:T(8,128)}, f32[1152,256]{0,1:T(8,128)}, u32[]{:S(2)}, u32[]{:S(2)}) collective-permute-start(f32[1152,256]{0,1:T(8,128)} %get-tuple-element.71), channel_id=1, source_target_pairs={{0,0},{1,16},{2,32},{3,48},{4,64},{5,80},{6,96},{7,112},{8,8},{9,2... | collective-permute-start | bytes 3538952 | tf_op jit(solution)/shard_map/ppermute | solution.py:32
  1086.7 239.3 %collective-permute-start.4 = (f32[1152,256]{0,1:T(8,128)}, f32[1152,256]{0,1:T(8,128)}, u32[]{:S(2)}, u32[]{:S(2)}) collective-permute-start(f32[1152,256]{0,1:T(8,128)} %get-tuple-element.71), channel_id=1, source_target_pairs={{0,8},{1,24},{2,40},{3,56},{4,72},{5,88},{6,104},{7,120},{8,0},{9,... | collective-permute-start | bytes 3538952 | tf_op jit(solution)/shard_map/ppermute | solution.py:33
  1088.8 61.4 %copy-start.20 = (f32[256,256]{1,0:T(8,128)S(1)}, f32[256,256]{1,0:T(8,128)}, u32[]{:S(2)}) copy-start(f32[256,256]{1,0:T(8,128)} %copy-done.19) | copy-start | bytes 786436
  1151.6 170.1 %copy-start.9 = (f32[1152,256]{0,1:T(8,128)S(1)}, f32[1152,256]{0,1:T(8,128)}, u32[]{:S(2)}) copy-start(f32[1152,256]{0,1:T(8,128)} %copy-done.8) | copy-start | bytes 3538948
  1152.2 163.1 %copy-start.17 = (f32[256,256]{1,0:T(8,128)}, f32[256,256]{1,0:T(8,128)S(1)}, u32[]{:S(2)}) copy-start(f32[256,256]{1,0:T(8,128)S(1)} %fusion.106) | copy-start | bytes 786436
  1316.7 7.1 copy-start.3
  1318.2 14.0 %slice-start = ((s8[10616832]{0:T(1024)(128)(4,1)}), s8[4194304]{0:T(1024)(128)(4,1)S(1)}, s32[]{:S(2)}) async-start(s8[10616832]{0:T(1024)(128)(4,1)} %bitcast.190), calls=%async_computation.7 | async-start | bytes 8388608
  1323.8 8.4 slice-start.1
  1326.0 2.0 copy-start.18
  1326.0 6.3 slice-start.2
Sparse Core Ops, SparseCore 0:
  13.3 144.8 all-reduce.13
  161.1 62.1 all-reduce.11
  314.3 297.8 all-reduce.19
  615.3 60.7 all-reduce.23
  779.1 131.4 all-reduce.15
  1016.5 62.9 all-reduce.21
  1084.2 231.1 all-reduce.17
where the time goes:
time: 1380 us; the launch traced here: 1370 us
  waiting for transfers between devices  835 us (61%)
  other arithmetic  255 us (18%)
  matrix products  185 us (13%)
  local copies, waits for them, and re-layouts  51.6 us (4%)
  starting transfers between devices  21.4 us (2%)
  between operations  20.9 us (2%)
    psum x2, waiting for transfers between devices, body(): gram0, top0 = lax.psum((g_loc, top_loc), ('row', 'col'))  430 us
    psum x2, waiting for transfers between devices, body(): gram, top = lax.psum((g_part, top_part), 'col')  170 us
    psum x1, waiting for transfers between devices, body(): curv = lax.psum(mm_tn(y_r, xp), ('row', 'col'))  163 us
    dot_general x23, matrix products, mm_nt(): return lax.dot_general(a, b, (((1,), (1,)), ((), ())), precision=HIGH)  108 us
    another operation x14, other arithmetic, small_factors(): second = jnp.linalg.cholesky(mm_nt(shifted, shifted))  76.6 us
    another operation x13, other arithmetic, small_factors(): low = jnp.linalg.cholesky(gram)  75.8 us
    dot_general x9, matrix products, mm(): return jnp.dot(a, b, precision=HIGH)  44.4 us
    another operation x4, other arithmetic, small_factors(): second_inv = jax.scipy.linalg.solve_triangular(second, identity, lower=True)  42.7 us
  transfers between devices with their start and end apart: 13, of which 9 were waited for; matrix products, arithmetic and copies ran while one was open for 20% of the time, Pallas kernels for 0%

commit v1 on v0

--- a/solution.py
+++ b/solution.py
@@ -97,7 +97,8 @@
             x_r, x_e = lax.psum((xp, ext), "col")
         else:
             x_r = lax.psum(xp, "col")
-        curv = lax.psum(mm_tn(y_r, xp), ("row", "col"))
+        one_axis = lax.psum(mm_tn(y_r, xp), "col")
+        curv = lax.psum(one_axis, "row")
         x_c = transpose_exchange(x_r, rows, cols)
         middle = mm_nt(mm(transform, curv), transform)
         w_r = mm_nt(x_r, transform) - 0.5 * mm(y_r, middle)

time: 1380 us -> 1230 us (0.89)
  waiting for transfers between devices: 835 us -> 713 us
    psum x2 -> x3, waiting for transfers between devices: 163 us -> 466 us  [the longest x2 270 us: body(): curv = lax.psum(one_axis, 'row')]
    psum x2 -> x1, waiting for transfers between devices: 430 us -> 142 us  [body(): gram0, top0 = lax.psum((g_loc, top_loc), ('row', 'col'))]
    psum x2, waiting for transfers between devices: 170 us -> 102 us  [body(): gram, top = lax.psum((g_part, top_part), 'col')]
    psum x1, waiting for transfers between devices: 41.3 us -> 2.12 us  [body(): colb = lax.psum(jnp.where(col_zero, a[:, :width], 0.0), 'col')]
    ppermute x3, waiting for transfers between devices: 18.9 us -> 0.01 us  [transpose_exchange(): got1 = lax.ppermute(x, both, first)]
  transfers between devices with their start and end apart: 13 -> 13, of which waited for: 9 -> 7; matrix products, arithmetic and copies ran while one was open for 20% -> 20% of each run, Pallas kernels for 0% -> 0%
where the time goes in v1:
time: 1230 us
  waiting for transfers between devices  713 us (58%)
  other arithmetic  245 us (20%)
  matrix products  182 us (15%)
  local copies, waits for them, and re-layouts  41.1 us (3%)
  starting transfers between devices  23.1 us (2%)
  between operations  21 us (2%)
    psum x2, waiting for transfers between devices, body(): curv = lax.psum(one_axis, 'row')  270 us
    psum x1, waiting for transfers between devices, body(): one_axis = lax.psum(mm_tn(y_r, xp), 'col')  197 us
    psum x1, waiting for transfers between devices, body(): gram0, top0 = lax.psum((g_loc, top_loc), ('row', 'col'))  142 us
    dot_general x23, matrix products, mm_nt(): return lax.dot_general(a, b, (((1,), (1,)), ((), ())), precision=HIGH)  109 us
    psum x2, waiting for transfers between devices, body(): gram, top = lax.psum((g_part, top_part), 'col')  102 us
    another operation x13, other arithmetic, small_factors(): low = jnp.linalg.cholesky(gram)  76 us
    another operation x14, other arithmetic, small_factors(): second = jnp.linalg.cholesky(mm_nt(shifted, shifted))  69.2 us
    dot_general x9, matrix products, mm(): return jnp.dot(a, b, precision=HIGH)  43.4 us
  transfers between devices with their start and end apart: 13, of which 7 were waited for; matrix products, arithmetic and copies ran while one was open for 20% of the time, Pallas kernels for 0%

profile of v1, /device:TPU:1, one launch (start us, length us, event | category | flops | bytes accessed | tf_op | source)
XLA Modules:
  0.0 1226.3 jit_solution(12731197977630868926)
XLA Ops:
  9.6 2.0 fusion.18
  13.3 1.9 copy.20
  19.9 142.4 %all-reduce.20.cloned.1.call-done = (f32[256,256]{0,1:T(8,128)}, f32[256,256]{0,1:T(8,128)}) async-done(((f32[256,256]{0,1:T(8,128)}, f32[256,256]{0,1:T(8,128)}), (f32[256,256]{0,1:T(8,128)}, f32[256,256]{0,1:T(8,128)})) %all-reduce.20.cloned.1.call-update) | async-done | bytes 524304 | tf_op jit(solution)/shard_map/psum | solution.py:68
  164.4 11.7 cholesky.214
  176.2 9.8 custom-call.17
  186.5 11.7 cholesky.231
  200.3 4.1 while.8
  204.4 19.7 %custom-call.18 = f32[2,128,128]{1,2,0:T(8,128)S(1)} custom-call(f32[2,128,128]{2,1,0:T(8,128)S(1)} %get-tuple-element.30), custom_call_target="InvertDiagBlocksLowerTriangular" | custom-call | tf_op jit(solution)/shard_map/jit(_solve_triangular)/triangular_solve | solution.py:43
  226.9 2.1 all-reduce.12.cloned.1.call-done
  229.0 7.2 collective-permute-start.1
  236.4 11.7 cholesky.248
  248.2 9.8 custom-call.19
  258.5 11.7 cholesky.265
  272.9 4.0 while.9
  276.9 20.7 %custom-call.20 = f32[2,128,128]{1,2,0:T(8,128)} custom-call(f32[2,128,128]{2,1,0:T(8,128)S(1)} %get-tuple-element.31), custom_call_target="InvertDiagBlocksLowerTriangular" | custom-call | tf_op jit(solution)/shard_map/jit(_solve_triangular)/triangular_solve | solution.py:46
  297.6 2.6 convolution_add_fusion.3
  300.3 2.8 broadcast_select_fusion.1
  303.2 4.2 convolution_add_fusion.1
  307.4 2.8 fusion.22
  310.3 19.2 %fusion.94 = f32[256,1152]{1,0:T(8,128)S(1)} fusion(f32[2304,256]{1,0:T(8,128)S(1)} %convolution_add_fusion.1, f32[1152,2304]{1,0:T(8,128)S(1)} %bitcast.193), kind=kOutput, calls=%fused_computation.198 | convolution fusion | flops 8153726976 | bytes 14155776 | tf_op jit(solution)/shard_map/dot_general | solution.py:12
  330.5 2.0 fusion.97
  336.8 2.3 fusion.96
  339.0 196.9 %all-reduce.24.cloned.1.call-done = (f32[256,256]{1,0:T(8,128)}, f32[1152,256]{0,1:T(8,128)}, f32[256,256]{1,0:T(8,128)}) async-done(((f32[256,256]{1,0:T(8,128)}, f32[1152,256]{0,1:T(8,128)}, f32[256,256]{1,0:T(8,128)}), (f32[256,256]{1,0:T(8,128)}, f32[1152,256]{0,1:T(8,128)}, f32[256,256]{1,0:T(8,128)})) %all-reduce.24.cloned.1.call-update) | async-done | bytes 1703952 | tf_op jit(solution)/shard_map/psum | solution.py:100
  536.0 7.1 collective-permute-start.3
  543.3 4.4 fusion.100
  548.8 167.1 %all-reduce.14.cloned.1.call-done = f32[256,256]{1,0:T(8,128)} async-done(((f32[256,256]{1,0:T(8,128)}), f32[256,256]{1,0:T(8,128)}) %all-reduce.14.cloned.1.call-update) | async-done | bytes 262160 | tf_op jit(solution)/shard_map/psum | solution.py:101
  718.9 2.0 fusion.4
  722.7 2.4 fusion.3
  725.1 2.1 convolution_multiply_fusion.1
  727.3 1.9 broadcast_select_fusion.6
  729.2 4.2 convolution_subtract_fusion.6
  733.5 2.3 fusion.102
  735.8 19.2 %convolution_subtract_fusion.3 = f32[1152,2304]{1,0:T(8,128)} fusion(f32[1152,2304]{1,0:T(8,128)S(1)} %bitcast.195, f32[1152,256]{0,1:T(8,128)S(1)} %convolution_add_fusion.3, f32[2304,256]{1,0:T(8,128)S(1)} %convolution_subtract_fusion.6), kind=kOutput, calls=%fused_computation.11 | convolution fusion | flops 8156381184 | bytes 24772608 | tf_op jit(solution)/shard_map/dot_general | solution.py:20
  755.0 2.6 fusion.1
  759.0 2.8 fusion.103
  761.9 14.0 %convolution_subtract_fusion.2 = f32[1152,2304]{1,0:T(8,128)} fusion(f32[1152,2304]{1,0:T(8,128)} %convolution_subtract_fusion.3, f32[1152,256]{1,0:T(8,128)} %copy-done.12, f32[2304,256]{1,0:T(8,128)S(1)} %convolution_add_fusion.1), kind=kOutput, calls=%fused_computation.10 | convolution fusion | flops 8156381184 | bytes 24772608 | tf_op jit(solution)/shard_map/dot_general | solution.py:20
  777.5 42.6 %all-reduce.16.cloned.1.call-done = f32[256,256]{0,1:T(8,128)} async-done(((f32[256,256]{0,1:T(8,128)}), f32[256,256]{0,1:T(8,128)}) %all-reduce.16.cloned.1.call-update) | async-done | bytes 262160 | tf_op jit(solution)/shard_map/psum | solution.py:86
  824.5 13.2 %cholesky.282 = f32[128,128]{1,0:T(8,128)} custom-call(f32[128,128]{1,0:T(8,128)} %cholesky.352), custom_call_target="Cholesky" | custom-call | tf_op jit(solution)/shard_map/jit(cholesky)/cholesky | solution.py:42
  839.9 11.3 custom-call.21
  856.2 13.2 %cholesky.299 = f32[128,128]{1,0:T(8,128)} custom-call(f32[128,128]{1,0:T(8,128)} %convolution_subtract_fusion.14), custom_call_target="Cholesky" | custom-call | tf_op jit(solution)/shard_map/jit(cholesky)/cholesky | solution.py:42
  875.3 6.9 while.10
  875.9 2.9 bitcast_dynamic-update-slice_fusion.10
  879.4 2.8 bitcast_dynamic-update-slice_fusion.10
  882.2 21.3 %custom-call.22 = f32[2,128,128]{1,2,0:T(8,128)} custom-call(f32[2,128,128]{2,1,0:T(8,128)} %get-tuple-element.32), custom_call_target="InvertDiagBlocksLowerTriangular" | custom-call | tf_op jit(solution)/shard_map/jit(_solve_triangular)/triangular_solve | solution.py:43
  907.8 4.4 convolution_add_fusion
  913.6 11.2 fusion.104
  926.2 2.6 convolution_add_fusion.2
  928.8 1.9 fusion.107
  932.3 3.1 copy.15
  935.4 59.4 %all-reduce.22.cloned.1.call-done = (f32[256,256]{0,1:T(8,128)}, f32[256,256]{1,0:T(8,128)}, f32[1152,256]{0,1:T(8,128)}) async-done(((f32[256,256]{0,1:T(8,128)}, f32[256,256]{1,0:T(8,128)}, f32[1152,256]{0,1:T(8,128)}), (f32[256,256]{0,1:T(8,128)}, f32[256,256]{1,0:T(8,128)}, f32[1152,256]{0,1:T(8,128)})) %all-reduce.22.cloned.1.call-update) | async-done | bytes 1703952 | tf_op jit(solution)/shard_map/psum | solution.py:86
  994.8 7.2 collective-permute-start.5
  1004.7 11.7 cholesky.316
  1017.1 9.8 custom-call.23
  1027.5 11.7 cholesky.333
  1041.1 3.9 while.11
  1045.1 19.8 %custom-call.24 = f32[2,128,128]{1,2,0:T(8,128)S(1)} custom-call(f32[2,128,128]{2,1,0:T(8,128)S(1)} %get-tuple-element.33), custom_call_target="InvertDiagBlocksLowerTriangular" | custom-call | tf_op jit(solution)/shard_map/jit(_solve_triangular)/triangular_solve | solution.py:46
  1067.7 4.5 fusion.110
  1072.3 102.4 %all-reduce.18.cloned.1.call-done = f32[256,256]{1,0:T(8,128)} async-done(((f32[256,256]{1,0:T(8,128)}), f32[256,256]{1,0:T(8,128)}) %all-reduce.18.cloned.1.call-update) | async-done | bytes 262160 | tf_op jit(solution)/shard_map/psum | solution.py:101
  1177.7 3.3 fusion.2
  1181.0 2.1 convolution_multiply_fusion
  1183.2 1.9 broadcast_select_fusion.4
  1185.1 4.3 convolution_subtract_fusion.4
  1189.4 18.1 %convolution_subtract_fusion.1 = f32[1152,2304]{1,0:T(8,128)S(1)} fusion(f32[1152,2304]{1,0:T(8,128)S(1)} %bitcast.191, f32[1152,256]{0,1:T(8,128)S(1)} %copy-done.9, f32[2304,256]{1,0:T(8,128)S(1)} %convolution_subtract_fusion.4), kind=kOutput, calls=%fused_computation.9 | convolution fusion | flops 8156381184 | bytes 24772608 | tf_op jit(solution)/shard_map/dot_general | solution.py:20
  1207.5 11.5 convolution_subtract_fusion
  (243 shorter events, 79.3 us)
Async XLA Ops:
  7.2 1.4 slice-start.9
  7.2 155.1 %all-reduce.20.cloned.1.call-start = ((), (), s32[]{:S(2)}) async-start(), calls=%async_computation.4 | async-start | bytes 1048576 | tf_op jit(solution)/shard_map/psum | solution.py:68
  11.6 1.7 slice-start.10
  11.7 217.4 %all-reduce.12.cloned.1.call-start = ((), (), s32[]{:S(2)}) async-start(), calls=%async_computation | async-start | bytes 4718592 | tf_op jit(solution)/shard_map/psum | solution.py:62
  16.8 519.1 %all-reduce.24.cloned.1.call-start = ((), (), s32[]{:S(2)}) async-start(), calls=%async_computation.6 | async-start | bytes 3407872 | tf_op jit(solution)/shard_map/psum | solution.py:100
  19.9 204.8 %copy-start.18 = (f32[256,256]{1,0:T(8,128)}, f32[256,256]{1,0:T(8,128)S(1)}, u32[]{:S(2)}) copy-start(f32[256,256]{1,0:T(8,128)S(1)} %fusion.39) | copy-start | bytes 786436
  163.4 61.7 %copy-start.33 = (f32[256,256]{0,1:T(8,128)S(1)}, f32[256,256]{0,1:T(8,128)}, u32[]{:S(2)}) copy-start(f32[256,256]{0,1:T(8,128)} %get-tuple-element.69) | copy-start | bytes 786436
  224.4 73.2 %copy-start.21 = (f32[128,256]{1,0:T(8,128)}, f32[128,256]{1,0:T(8,128)S(1)}, u32[]{:S(2)}) copy-start(f32[128,256]{1,0:T(8,128)S(1)} %fusion.46) | copy-start | bytes 393220
  225.0 72.6 %copy-start.26 = (f32[128,256]{1,0:T(8,128)}, f32[128,256]{1,0:T(8,128)S(1)}, u32[]{:S(2)}) copy-start(f32[128,256]{1,0:T(8,128)S(1)} %fusion.61) | copy-start | bytes 393220
  225.6 0.7 copy-start.10
  229.0 71.2 %collective-permute-start.1 = (f32[1152,512]{0,1:T(8,128)}, f32[1152,512]{0,1:T(8,128)}, u32[]{:S(2)}, u32[]{:S(2)}) collective-permute-start(f32[1152,512]{0,1:T(8,128)} %all-reduce.12.cloned.1.call-done), channel_id=1, source_target_pairs={{0,0},{1,16},{2,32},{3,48},{4,64},{5,80},{6,96},{7,112},{8,8},{9,2... | collective-permute-start | bytes 7077896 | tf_op jit(solution)/shard_map/ppermute | solution.py:32
  236.2 64.0 %collective-permute-start = (f32[1152,512]{0,1:T(8,128)}, f32[1152,512]{0,1:T(8,128)}, u32[]{:S(2)}, u32[]{:S(2)}) collective-permute-start(f32[1152,512]{0,1:T(8,128)} %all-reduce.12.cloned.1.call-done), channel_id=1, source_target_pairs={{0,8},{1,24},{2,40},{3,56},{4,72},{5,88},{6,104},{7,120},{8,0},{9,... | collective-permute-start | bytes 7077896 | tf_op jit(solution)/shard_map/ppermute | solution.py:33
  276.9 26.3 %copy-start.30 = (f32[256,256]{1,0:T(8,128)}, f32[256,256]{1,0:T(8,128)S(1)}, u32[]{:S(2)}) copy-start(f32[256,256]{1,0:T(8,128)S(1)} %get-tuple-element.327) | copy-start | bytes 786436
  276.9 26.3 %copy-start.40 = (s32[2,2]{1,0:T(2,128)}, s32[2,2]{1,0:T(2,128)S(1)}, u32[]{:S(2)}) copy-start(s32[2,2]{1,0:T(2,128)S(1)} %get-tuple-element.363) | copy-start | bytes 52
  300.2 3.0 copy-start.22
  300.2 3.0 copy-start.27
  300.2 3.0 copy-start.37
  300.3 10.0 slice-start.3
  300.3 10.0 slice-start.4
  303.2 4.3 copy-start.4
  303.2 4.3 copy-start.6
  303.2 7.1 slice-start.5
  329.5 1.0 copy-start.13
  332.5 383.4 %all-reduce.14.cloned.1.call-start = ((), (), s32[]{:S(2)}) async-start(), calls=%async_computation.1 | async-start | bytes 524288 | tf_op jit(solution)/shard_map/psum | solution.py:101
  536.0 191.3 %collective-permute-start.3 = (f32[1152,256]{0,1:T(8,128)}, f32[1152,256]{0,1:T(8,128)}, u32[]{:S(2)}, u32[]{:S(2)}) collective-permute-start(f32[1152,256]{0,1:T(8,128)} %get-tuple-element.74), channel_id=1, source_target_pairs={{0,0},{1,16},{2,32},{3,48},{4,64},{5,80},{6,96},{7,112},{8,8},{9,2... | collective-permute-start | bytes 3538952 | tf_op jit(solution)/shard_map/ppermute | solution.py:32
  543.1 184.2 %collective-permute-start.2 = (f32[1152,256]{0,1:T(8,128)}, f32[1152,256]{0,1:T(8,128)}, u32[]{:S(2)}, u32[]{:S(2)}) collective-permute-start(f32[1152,256]{0,1:T(8,128)} %get-tuple-element.74), channel_id=1, source_target_pairs={{0,8},{1,24},{2,40},{3,56},{4,72},{5,88},{6,104},{7,120},{8,0},{9,... | collective-permute-start | bytes 3538952 | tf_op jit(solution)/shard_map/ppermute | solution.py:33
  543.2 276.9 %all-reduce.16.cloned.1.call-start = ((), (), s32[]{:S(2)}) async-start(), calls=%async_computation.2 | async-start | bytes 524288 | tf_op jit(solution)/shard_map/psum | solution.py:86
  543.3 4.4 copy-start.14
  543.3 4.4 copy-start.34
  715.9 3.0 copy-start.20
  717.4 3.5 copy-start.11
  717.4 3.5 copy-start.31
  718.9 2.5 copy-start.25
  720.9 1.8 copy-start.12
  721.0 1.8 copy-start.39
  725.1 10.7 slice-start.6
  727.2 2.0 copy-start.15
  727.2 8.5 slice-start.7
  729.2 6.6 slice-start.8
  735.8 19.2 %copy-start.5 = (f32[1152,512]{0,1:T(8,128)S(1)}, f32[1152,512]{0,1:T(8,128)}, u32[]{:S(2)}) copy-start(f32[1152,512]{0,1:T(8,128)} %copy-done.4) | copy-start | bytes 7077892
  735.8 19.2 %copy-start.7 = (f32[1152,512]{0,1:T(8,128)S(1)}, f32[1152,512]{0,1:T(8,128)}, u32[]{:S(2)}) copy-start(f32[1152,512]{0,1:T(8,128)} %copy-done.6) | copy-start | bytes 7077892
  735.8 19.2 %copy-start.38 = (pred[2304]{0:T(1024)(128)(4,1)S(1)}, pred[2304]{0:T(1024)(128)(4,1)}, u32[]{:S(2)}) copy-start(pred[2304]{0:T(1024)(128)(4,1)} %get-tuple-element.120) | copy-start | bytes 6916
  757.6 1.4 copy-start
  761.8 232.9 %all-reduce.22.cloned.1.call-start = ((), (), s32[]{:S(2)}) async-start(), calls=%async_computation.5 | async-start | bytes 3407872 | tf_op jit(solution)/shard_map/psum | solution.py:86
  775.9 99.4 %copy-start.41 = (s32[2,2]{1,0:T(2,128)S(1)}, s32[2,2]{1,0:T(2,128)}, u32[]{:S(2)}) copy-start(s32[2,2]{1,0:T(2,128)} %copy-done.40) | copy-start | bytes 52
  822.0 85.8 %copy-start.1 = (f32[2304,256]{0,1:T(8,128)S(1)}, f32[2304,256]{0,1:T(8,128)}, u32[]{:S(2)}) copy-start(f32[2304,256]{0,1:T(8,128)} %copy-done) | copy-start | bytes 7077892
  822.0 85.8 %copy-start.35 = (s32[2304]{0:T(1024)S(1)}, s32[2304]{0:T(1024)}, u32[]{:S(2)}) copy-start(s32[2304]{0:T(1024)} %get-tuple-element.118) | copy-start | bytes 27652
  904.7 2.4 copy-start.23
  912.2 1.4 copy-start.2
  924.7 1.4 copy-start.36
  928.8 3.5 copy-start.8
  930.7 244.0 %all-reduce.18.cloned.1.call-start = ((), (), s32[]{:S(2)}) async-start(), calls=%async_computation.3 | async-start | bytes 524288 | tf_op jit(solution)/shard_map/psum | solution.py:101
  932.3 70.1 %copy-start.24 = (f32[128,256]{1,0:T(8,128)S(1)}, f32[128,256]{1,0:T(8,128)}, u32[]{:S(2)}) copy-start(f32[128,256]{1,0:T(8,128)} %copy-done.23) | copy-start | bytes 393220
  932.3 70.2 %copy-start.29 = (f32[128,256]{1,0:T(8,128)S(1)}, f32[128,256]{1,0:T(8,128)}, u32[]{:S(2)}) copy-start(f32[128,256]{1,0:T(8,128)} %copy-done.28) | copy-start | bytes 393220
  994.8 188.4 %collective-permute-start.5 = (f32[1152,256]{0,1:T(8,128)}, f32[1152,256]{0,1:T(8,128)}, u32[]{:S(2)}, u32[]{:S(2)}) collective-permute-start(f32[1152,256]{0,1:T(8,128)} %get-tuple-element.72), channel_id=1, source_target_pairs={{0,0},{1,16},{2,32},{3,48},{4,64},{5,80},{6,96},{7,112},{8,8},{9,2... | collective-permute-start | bytes 3538952 | tf_op jit(solution)/shard_map/ppermute | solution.py:32
  1002.0 181.2 %collective-permute-start.4 = (f32[1152,256]{0,1:T(8,128)}, f32[1152,256]{0,1:T(8,128)}, u32[]{:S(2)}, u32[]{:S(2)}) collective-permute-start(f32[1152,256]{0,1:T(8,128)} %get-tuple-element.72), channel_id=1, source_target_pairs={{0,8},{1,24},{2,40},{3,56},{4,72},{5,88},{6,104},{7,120},{8,0},{9,... | collective-permute-start | bytes 3538952 | tf_op jit(solution)/shard_map/ppermute | solution.py:33
  1004.1 60.8 %copy-start.19 = (f32[256,256]{1,0:T(8,128)S(1)}, f32[256,256]{1,0:T(8,128)}, u32[]{:S(2)}) copy-start(f32[256,256]{1,0:T(8,128)} %copy-done.18) | copy-start | bytes 786436
  1066.4 111.2 %copy-start.9 = (f32[1152,256]{0,1:T(8,128)S(1)}, f32[1152,256]{0,1:T(8,128)}, u32[]{:S(2)}) copy-start(f32[1152,256]{0,1:T(8,128)} %copy-done.8) | copy-start | bytes 3538948
  1067.0 0.7 copy-start.16
  1067.7 113.3 %copy-start.3 = (f32[2304,256]{1,0:T(8,128)S(1)}, f32[2304,256]{1,0:T(8,128)}, u32[]{:S(2)}) copy-start(f32[2304,256]{1,0:T(8,128)} %copy-done.2) | copy-start | bytes 7077892
  1174.7 14.7 %slice-start = ((s8[10616832]{0:T(1024)(128)(4,1)}), s8[4194304]{0:T(1024)(128)(4,1)S(1)}, s32[]{:S(2)}) async-start(s8[10616832]{0:T(1024)(128)(4,1)} %bitcast.190), calls=%async_computation.7 | async-start | bytes 8388608
  1181.0 8.4 slice-start.1
  1183.1 2.0 copy-start.17
  1183.1 6.3 slice-start.2
  (2 other events, 1.3 us)
Sparse Core Ops, SparseCore 0:
  13.5 148.7 all-reduce.19
  165.4 63.6 all-reduce.11
  332.6 203.3 all-reduce.23
  543.3 172.5 all-reduce.13
  761.9 58.1 all-reduce.15
  930.9 63.8 all-reduce.21
  1004.2 170.4 all-reduce.17
